TPU v7x, 32 devices: a whole 2x2x4 slice. The times are simulated.
32 devices in a mesh: head: 4 (over y, x), batch: 8 (over z, core).
Axes of the slice: x: 2, y: 2, z: 4, core: 2. Of those that a mesh axis runs over, the one named last changes fastest.
Arguments:
- hidden_in: bfloat16 [8, 256, 4096], P('batch', None, 'head')
- w_query: bfloat16 [4096, 4096], P('batch', 'head'), may hold values from -0.09375 to 0.09375
- w_key: bfloat16 [4096, 4096], P('batch', 'head'), may hold values from -0.09375 to 0.09375
- w_value: bfloat16 [4096, 4096], P('batch', 'head'), may hold values from -0.09375 to 0.09375
- w_beta: bfloat16 [4096, 32], P('batch', 'head'), may hold values from -0.09375 to 0.09375
- w_out: bfloat16 [4096, 4096], P('head', 'batch'), may hold values from -0.125 to 0.125
- mem_pos: int32 [8, 2, 64], P('batch'), may hold values from 0 to 127, as said below
- memory_in: float32 [8, 32, 128, 128], P('batch', 'head'), may hold values from -6 to 6
Outputs:
- hidden_out: bfloat16 [8, 256, 4096], P('batch', None, 'head')
- memory_out: float32 [8, 32, 128, 128], P('batch', 'head')
Inputs may be any that keep to these rules, and one draw needn't show every extreme that they name: `mem_pos`: within each sequence and segment the 64 positions are distinct and ascending.
All inputs are finite; a program needn't handle non-finite values.
Results may differ from a plain program's by a relative error of at most 0.005.
Values may be sent and summed in bfloat16 or wider, within the bound.
No kernel may reach another device: no remote copies, remote signals or barrier semaphores. Data moves between devices by JAX's collectives and lax.ppermute only.
A program may use at most 128 MiB of HBM per device.

v0:
```python
import jax
import jax.numpy as jnp
from jax import lax
from jax.sharding import PartitionSpec as P

SEGS = 2
epsilon = 1e-05


def recur(query, keys, values, beta, state):
    highest = lax.Precision.HIGHEST
    readouts = []
    for segment in range(query.shape[1]):
        readouts.append(
            jnp.einsum("bhij,blhj->blhi", state, query[:, segment], precision=highest).astype(
                jnp.bfloat16
            )
        )
        recalled = jnp.einsum("bhij,bmhj->bmhi", state, keys[:, segment], precision=highest)
        change = beta[:, segment][..., None] * (values[:, segment] - recalled)
        state = state + jnp.einsum("bmhi,bmhj->bhij", change, keys[:, segment], precision=highest)
    return (jnp.stack(readouts, axis=1), state)


def body(hidden_in, w_query, w_key, w_value, w_beta, w_out, mem_pos, memory_in):
    seq_count, row_count, local_width = hidden_in.shape
    seg_rows = row_count // SEGS
    mem_count = mem_pos.shape[2]
    local_heads = w_beta.shape[1]
    local_features = w_query.shape[1]
    head_size = local_features // local_heads
    x_float = hidden_in.astype(jnp.float32)
    whole = lax.all_gather(hidden_in, "head", axis=2, tiled=True)
    whole_float = whole.astype(jnp.float32)
    mean_square = jnp.mean(whole_float * whole_float, axis=2, keepdims=True)
    normed = (whole_float * lax.rsqrt(mean_square + epsilon)).astype(jnp.bfloat16)
    full_width = normed.shape[2]
    offsets = (jnp.arange(SEGS, dtype=jnp.int32) * seg_rows)[None, :, None]
    picked = (mem_pos + offsets).reshape(seq_count, SEGS * mem_count)
    memory_rows = jax.vmap(lambda block, where: jnp.take(block, where, axis=0))(normed, picked)
    memory_rows = memory_rows.reshape(seq_count * SEGS * mem_count, full_width)
    token_rows = normed.reshape(seq_count * row_count, full_width)
    piece_query = lax.all_gather(w_query, "batch", axis=0, tiled=True)
    piece_key = lax.all_gather(w_key, "batch", axis=0, tiled=True)
    piece_value = lax.all_gather(w_value, "batch", axis=0, tiled=True)
    piece_beta = lax.all_gather(w_beta, "batch", axis=0, tiled=True)
    query = jnp.dot(token_rows, piece_query, preferred_element_type=jnp.float32)
    keys = jnp.dot(memory_rows, piece_key, preferred_element_type=jnp.float32)
    values = jnp.dot(memory_rows, piece_value, preferred_element_type=jnp.float32)
    logits = jnp.dot(memory_rows, piece_beta, preferred_element_type=jnp.float32)
    query = (query * head_size ** (-0.5)).reshape(seq_count, SEGS, seg_rows, local_heads, head_size)
    keys = keys.reshape(seq_count, SEGS, mem_count, local_heads, head_size)
    keys = keys * lax.rsqrt(jnp.sum(keys * keys, axis=-1, keepdims=True) + 1e-06)
    values = values.reshape(seq_count, SEGS, mem_count, local_heads, head_size)
    beta = jax.nn.sigmoid(logits).reshape(seq_count, SEGS, mem_count, local_heads)
    readout, state = recur(query, keys, values, beta, memory_in)
    readout = readout.reshape(seq_count * row_count, local_features)
    terms = jnp.dot(
        readout,
        lax.all_gather(w_out, "batch", axis=1, tiled=True),
        preferred_element_type=jnp.float32,
    )
    mixed = lax.psum_scatter(terms, "head", scatter_dimension=1, tiled=True)
    hidden_out = (mixed + x_float.reshape(seq_count * row_count, local_width)).astype(jnp.bfloat16)
    return (hidden_out.reshape(hidden_in.shape), state)


def solution(mesh):
    in_specs = (
        P("batch", None, "head"),
        P("batch", "head"),
        P("batch", "head"),
        P("batch", "head"),
        P("batch", "head"),
        P("head", "batch"),
        P("batch", None, None),
        P("batch", "head", None, None),
    )
    out_specs = (P("batch", None, "head"), P("batch", "head", None, None))
    return jax.shard_map(body, mesh=mesh, in_specs=in_specs, out_specs=out_specs, check_vma=False)
```

profile of v0, /device:TPU:0, one launch (start us, length us, event | category | flops | bytes accessed | tf_op | source)
XLA Modules:
  0.0 445.6 jit_solution(10736198151364103323)
XLA Ops:
  7.2 0.7 all-gather.6.cloned.1.call-update
  7.9 0.7 all-gather.12.cloned.1.call-update
  8.7 0.7 all-gather.10.cloned.1.call-update
  9.4 0.5 all-gather.8.cloned.1.call-update
  10.0 0.5 all-gather.14.cloned.1.call-update
  10.6 0.8 broadcast_add_fusion
  11.5 15.9 %all_gather.20 = bf16[4096,8]{0,1:T(8,128)(2,1)S(1)} all-gather(bf16[512,8]{0,1:T(8,128)(2,1)} %param.12), channel_id=1, replica_groups=mesh['head'=4,'batch'=8] {'batch'}, dimensions={0}, use_global_device_ids=true | all-gather | bytes 73728 | tf_op jit(solution)/shard_map/all_gather | solution.py:46
  27.4 20.3 %all-gather.6.cloned.1.call-done = bf16[1,256,4096]{2,1,0:T(8,128)(2,1)} async-done(((bf16[1,256,1024]{2,1,0:T(8,128)(2,1)}), bf16[1,256,4096]{2,1,0:T(8,128)(2,1)}) %all-gather.6.cloned.1.call-update) | async-done | bytes 2097168 | tf_op jit(solution)/shard_map/all_gather | solution.py:33
  47.8 2.1 fusion
  49.8 2.2 fusion.1
  52.0 3.7 gather_fusion
  55.8 0.4 fusion.22
  56.3 1.2 bitcast_select_fusion
  57.5 73.9 %all-gather.12.cloned.1.call-done = bf16[4096,1024]{1,0:T(8,128)(2,1)} async-done(((bf16[512,1024]{1,0:T(8,128)(2,1)}), bf16[4096,1024]{1,0:T(8,128)(2,1)}) %all-gather.12.cloned.1.call-update) | async-done | bytes 8388624 | tf_op jit(solution)/shard_map/all_gather | solution.py:44
  131.4 4.7 %convolution_bitcast_fusion.2 = f32[16,8,8,128]{3,1,2,0:T(8,128)S(1)} fusion(bf16[4096,1024]{1,0:T(8,128)(2,1)} %all-gather.12.cloned.1.call-done, bf16[128,4096]{1,0:T(8,128)(2,1)S(1)} %gather_fusion, pred[128]{0:T(512)(128)(4,1)S(1)} %compare_and_fusion), kind=kOutput, calls=%fused_computation.11 | convolution fusion | flops 1074266112 | bytes 9961600 | tf_op jit(solution)/shard_map/dot_general | solution.py:48
  136.2 0.2 multiply_reduce_fusion
  136.5 77.1 %all-gather.10.cloned.1.call-done = bf16[4096,1024]{1,0:T(8,128)(2,1)} async-done(((bf16[512,1024]{1,0:T(8,128)(2,1)}), bf16[4096,1024]{1,0:T(8,128)(2,1)}) %all-gather.10.cloned.1.call-update) | async-done | bytes 8388624 | tf_op jit(solution)/shard_map/all_gather | solution.py:45
  213.6 12.1 %copy.27 = bf16[1024,4096]{1,0:T(8,128)(2,1)} copy(bf16[1024,4096]{0,1:T(8,128)(2,1)} %bitcast.131) | data formatting | bytes 16777216 | tf_op jit(solution)/shard_map/dot_general | solution.py:49
  225.7 69.9 %all-gather.8.cloned.1.call-done = bf16[4096,1024]{1,0:T(8,128)(2,1)} async-done(((bf16[512,1024]{1,0:T(8,128)(2,1)}), bf16[4096,1024]{1,0:T(8,128)(2,1)}) %all-gather.8.cloned.1.call-update) | async-done | bytes 8388624 | tf_op jit(solution)/shard_map/all_gather | solution.py:43
  295.6 5.9 %fusion.7 = f32[32,8,8,128]{3,1,2,0:T(8,128)S(1)} fusion(bf16[4096,1024]{1,0:T(8,128)(2,1)} %all-gather.8.cloned.1.call-done, bf16[1,256,4096]{2,1,0:T(8,128)(2,1)S(1)} %fusion.1), kind=kOutput, calls=%fused_computation.8 | convolution fusion | flops 2147745792 | bytes 11534336 | tf_op jit(solution)/shard_map/dot_general | solution.py:47
  301.7 1.2 fusion.12
  303.2 2.9 convolution_bitcast_fusion.3
  306.1 1.1 fusion.17
  307.2 1.0 fusion.10
  308.3 1.2 fusion.13
  309.6 0.3 copy.30
  309.9 67.7 %all-gather.14.cloned.1.call-done = bf16[1024,4096]{1,0:T(8,128)(2,1)} async-done(((bf16[1024,512]{1,0:T(8,128)(2,1)}), bf16[1024,4096]{1,0:T(8,128)(2,1)}) %all-gather.14.cloned.1.call-update) | async-done | bytes 8388624 | tf_op jit(solution)/shard_map/all_gather | solution.py:60
  377.6 7.7 %fusion.25 = f32[256,4096]{1,0:T(8,128)} fusion(bf16[1024,4096]{1,0:T(8,128)(2,1)} %all-gather.14.cloned.1.call-done, bf16[32,8,8,128]{3,2,1,0:T(8,128)(2,1)S(1)} %bitcast.136), kind=kOutput, calls=%fused_computation.36 | convolution fusion | flops 2147483648 | bytes 13107200 | tf_op jit(solution)/shard_map/dot_general | solution.py:58
  385.4 1.1 fusion.19
  386.5 1.8 fusion.11
  388.3 48.3 %reduce-scatter.2.cloned.1.call-done = f32[256,1024]{1,0:T(8,128)} async-done(((f32[256,4096]{1,0:T(8,128)}), f32[256,1024]{1,0:T(8,128)}) %reduce-scatter.2.cloned.1.call-update) | async-done | bytes 1048592 | tf_op jit(solution)/shard_map/reduce_scatter | solution.py:63
  436.6 2.2 fusion.24
  (32 shorter events, 1.3 us)
Async XLA Ops:
  7.2 40.6 %all-gather.6.cloned.1.call-start = ((), (), s32[]{:S(2)}) async-start(), calls=%async_computation.1 | async-start | bytes 2621440 | tf_op jit(solution)/shard_map/all_gather | solution.py:33
  7.9 123.5 %all-gather.12.cloned.1.call-start = ((), (), s32[]{:S(2)}) async-start(), calls=%async_computation.4 | async-start | bytes 9437184 | tf_op jit(solution)/shard_map/all_gather | solution.py:44
  8.6 204.9 %all-gather.10.cloned.1.call-start = ((), (), s32[]{:S(2)}) async-start(), calls=%async_computation.3 | async-start | bytes 9437184 | tf_op jit(solution)/shard_map/all_gather | solution.py:45
  9.4 286.2 %all-gather.8.cloned.1.call-start = ((), (), s32[]{:S(2)}) async-start(), calls=%async_computation.2 | async-start | bytes 9437184 | tf_op jit(solution)/shard_map/all_gather | solution.py:43
  10.0 367.6 %all-gather.14.cloned.1.call-start = ((), (), s32[]{:S(2)}) async-start(), calls=%async_computation.5 | async-start | bytes 9437184 | tf_op jit(solution)/shard_map/all_gather | solution.py:60
  10.5 426.0 %reduce-scatter.2.cloned.1.call-start = ((), (), s32[]{:S(2)}) async-start(), calls=%async_computation.6 | async-start | bytes 5242880 | tf_op jit(solution)/shard_map/reduce_scatter | solution.py:63
  225.7 76.1 %copy-start.1 = (f32[1,8,128,128]{3,2,1,0:T(8,128)S(1)}, f32[1,8,128,128]{3,2,1,0:T(8,128)}, u32[]{:S(2)}) copy-start(f32[1,8,128,128]{3,2,1,0:T(8,128)} %param.15) | copy-start | bytes 1572868
  295.6 7.6 %copy-start = (bf16[1024,4096]{1,0:T(8,128)(2,1)S(1)}, bf16[1024,4096]{1,0:T(8,128)(2,1)}, u32[]{:S(2)}) copy-start(bf16[1024,4096]{1,0:T(8,128)(2,1)} %copy.27) | copy-start | bytes 25165828
  295.6 7.6 %copy-start.2 = (bf16[1,128,1,1,1,1,4096]{6,1,5,4,3,2,0:T(8,128)(2,1)S(1)}, bf16[1,128,1,1,1,1,4096]{6,1,5,4,3,2,0:T(8,128)(2,1)}, u32[]{:S(2)}) copy-start(bf16[1,128,1,1,1,1,4096]{6,1,5,4,3,2,0:T(8,128)(2,1)} %bitcast_select_fusion) | copy-start | bytes 3145732
  377.6 59.0 %copy-start.3 = (bf16[1,256,1024]{2,1,0:T(8,128)(2,1)S(1)}, bf16[1,256,1024]{2,1,0:T(8,128)(2,1)}, u32[]{:S(2)}) copy-start(bf16[1,256,1024]{2,1,0:T(8,128)(2,1)} %param.8) | copy-start | bytes 1572868
Sparse Core Ops, SparseCore 0:
  9.8 37.8 all-gather.5
  49.3 82.0 all-gather.11
  133.0 80.5 all-gather.9
  215.0 80.5 all-gather.7
  297.0 80.5 all-gather.13
  385.5 51.0 reduce-scatter.1
where the time goes:
time: 446 us
  waiting for transfers between devices  360 us (81%)
  matrix products  29.1 us (7%)
  local copies, waits for them, and re-layouts  16.9 us (4%)
  blocking collectives  15.9 us (4%)
  between operations  14.3 us (3%)
  other arithmetic  8.83 us (2%)
    all_gather x1, waiting for transfers between devices, body(): piece_value = lax.all_gather(w_value, 'batch', axis=0, tiled=True)  77.1 us
    all_gather x1, waiting for transfers between devices, body(): piece_key = lax.all_gather(w_key, 'batch', axis=0, tiled=True)  73.9 us
    all_gather x1, waiting for transfers between devices, body(): piece_query = lax.all_gather(w_query, 'batch', axis=0, tiled=True)  69.9 us
    all_gather x1, waiting for transfers between devices, body(): lax.all_gather(w_out, 'batch', axis=1, tiled=True)  67.7 us
    reduce_scatter x1, waiting for transfers between devices, body(): mixed = lax.psum_scatter(terms, 'head', scatter_dimension=1, tiled=True)  48.3 us
    all_gather x1, waiting for transfers between devices, body(): whole = lax.all_gather(hidden_in, 'head', axis=2, tiled=True)  20.3 us
    all_gather x1, blocking collectives, body(): piece_beta = lax.all_gather(w_beta, 'batch', axis=0, tiled=True)  15.9 us
    dot_general x1, local copies, waits for them, and re-layouts, body(): jnp.dot(memory_rows, piece_value, preferred_element_type=jnp.float32)  12.1 us
  transfers between devices with their start and end apart: 6, of which 6 were waited for; matrix products, arithmetic and copies ran while one was open for 10% of the time, Pallas kernels for 0%

commit v1 on v0

--- a/solution.py
+++ b/solution.py
@@ -41,7 +41,17 @@
     memory_rows = memory_rows.reshape(seq_count * SEGS * mem_count, full_width)
     token_rows = normed.reshape(seq_count * row_count, full_width)
     piece_query = lax.all_gather(w_query, "batch", axis=0, tiled=True)
-    piece_key = lax.all_gather(w_key, "batch", axis=0, tiled=True)
+
+    def cover_case(block_here, mesh_dim="batch"):
+        so_far_all = []
+        full_n = lax.axis_size(mesh_dim)
+        for jj in range(block_here.ndim):
+            so_far_all.append(full_n if jj == 0 else 1)
+        return lax.all_to_all(
+            jnp.tile(block_here, so_far_all), mesh_dim, split_axis=0, concat_axis=0, tiled=True
+        )
+
+    piece_key = cover_case(w_key)
     piece_value = lax.all_gather(w_value, "batch", axis=0, tiled=True)
     piece_beta = lax.all_gather(w_beta, "batch", axis=0, tiled=True)
     query = jnp.dot(token_rows, piece_query, preferred_element_type=jnp.float32)

time: 446 us -> 494 us (1.11)
  blocking collectives: 15.9 us -> 320 us
  waiting for transfers between devices: 360 us -> 89.7 us
  local copies, waits for them, and re-layouts: 16.9 us -> 24 us
  starting transfers between devices: 0.23 us -> 6.67 us
    all_gather x1, blocking collectives: 15.9 us -> 320 us  [body(): piece_beta = lax.all_gather(w_beta, 'batch', axis=0, tiled=True)]
    all_gather x1, waiting for transfers between devices: 77.1 us -> 0.01 us  [body(): piece_value = lax.all_gather(w_value, 'batch', axis=0, tiled=True)]
    all_gather x1 -> x0, waiting for transfers between devices: 73.9 us -> none  [body(): piece_key = lax.all_gather(w_key, 'batch', axis=0, tiled=True)]
    all_gather x1, waiting for transfers between devices: 69.9 us -> 0.01 us  [body(): piece_query = lax.all_gather(w_query, 'batch', axis=0, tiled=True)]
    all_gather x1, waiting for transfers between devices: 67.7 us -> 38.7 us  [body(): lax.all_gather(w_out, 'batch', axis=1, tiled=True)]
    all_gather x1, waiting for transfers between devices: 20.3 us -> 0.02 us  [body(): whole = lax.all_gather(hidden_in, 'head', axis=2, tiled=True)]
    all_to_all x0 -> x1, starting transfers between devices: none -> 6.49 us  [cover_case(): lax.all_to_all(jnp.tile(block_here, so_far_all), mesh_dim, split_axis=0,...]
    another operation x0 -> x1, local copies, waits for them, and re-layouts: none -> 5.53 us  [cover_case(): jnp.tile(block_here, so_far_all)]
  transfers between devices with their start and end apart: 6 -> 6, of which waited for: 6 -> 2; matrix products, arithmetic and copies ran while one was open for 10% -> 11% of each run, Pallas kernels for 0% -> 0%
where the time goes in v1:
time: 494 us; the launch traced here: 493 us
  blocking collectives  320 us (65%)
  waiting for transfers between devices  89.7 us (18%)
  matrix products  30.5 us (6%)
  local copies, waits for them, and re-layouts  24 us (5%)
  between operations  14 us (3%)
  other arithmetic  8.45 us (2%)
  starting transfers between devices  6.67 us (1%)
    all_gather x1, blocking collectives, body(): piece_beta = lax.all_gather(w_beta, 'batch', axis=0, tiled=True)  320 us
    reduce_scatter x1, waiting for transfers between devices, body(): mixed = lax.psum_scatter(terms, 'head', scatter_dimension=1, tiled=True)  48.3 us
    all_gather x1, waiting for transfers between devices, body(): lax.all_gather(w_out, 'batch', axis=1, tiled=True)  38.7 us
    dot_general x1, local copies, waits for them, and re-layouts, body(): jnp.dot(memory_rows, piece_value, preferred_element_type=jnp.float32)  11.8 us
  transfers between devices with their start and end apart: 6, of which 2 were waited for; matrix products, arithmetic and copies ran while one was open for 11% of the time, Pallas kernels for 0%

profile of v1, /device:TPU:0, one launch (start us, length us, event | category | flops | bytes accessed | tf_op | source)
XLA Modules:
  0.0 493.0 jit_solution(11289746915705233616)
XLA Ops:
  7.2 0.7 all-gather.5.cloned.1.call-update
  7.9 0.7 all-gather.9.cloned.1.call-update
  8.7 0.7 all-gather.7.cloned.1.call-update
  9.4 5.5 %tile.2 = bf16[8,512,1024]{2,1,0:T(8,128)(2,1)} broadcast(bf16[512,1024]{1,0:T(8,128)(2,1)} %param.10), dimensions={1,2} | broadcast | bytes 9437184 | tf_op jit(solution)/shard_map/tile | solution.py:51
  14.9 6.5 %all-to-all-start = ((bf16[8,512,1024]{2,1,0:T(8,128)(2,1)}), bf16[8,512,1024]{2,1,0:T(8,128)(2,1)}, u32[]{:S(2)}, u32[]{:S(2)}) async-start(bf16[8,512,1024]{2,1,0:T(8,128)(2,1)} %tile.2), calls=%async_computation | async-start | bytes 16777216 | tf_op jit(solution)/shard_map/all_to_all | solution.py:50
  21.4 0.5 all-gather.11.cloned.1.call-update
  22.3 319.7 %all_gather.17 = bf16[4096,8]{0,1:T(8,128)(2,1)S(1)} all-gather(bf16[512,8]{0,1:T(8,128)(2,1)S(1)} %copy-done.5), channel_id=1, replica_groups=mesh['head'=4,'batch'=8] {'batch'}, dimensions={0}, use_global_device_ids=true | all-gather | bytes 73728 | tf_op jit(solution)/shard_map/all_gather | solution.py:56
  342.1 2.1 fusion
  344.2 2.2 fusion.1
  346.4 4.7 gather_fusion
  351.1 1.8 fusion.22
  353.0 1.5 bitcast_select_fusion
  354.4 4.6 convolution_bitcast_fusion.2
  359.1 0.1 copy.35
  359.2 0.8 copy-done.2
  360.0 0.2 multiply_reduce_fusion
  360.3 11.8 %copy.27 = bf16[1024,4096]{1,0:T(8,128)(2,1)} copy(bf16[1024,4096]{0,1:T(8,128)(2,1)} %bitcast.136) | data formatting | bytes 16777216 | tf_op jit(solution)/shard_map/dot_general | solution.py:59
  372.1 5.9 %fusion.7 = f32[32,8,8,128]{3,1,2,0:T(8,128)S(1)} fusion(bf16[4096,1024]{1,0:T(8,128)(2,1)} %all-gather.7.cloned.1.call-done, bf16[1,256,4096]{2,1,0:T(8,128)(2,1)S(1)} %fusion.1), kind=kOutput, calls=%fused_computation.8 | convolution fusion | flops 2147745792 | bytes 11534336 | tf_op jit(solution)/shard_map/dot_general | solution.py:57
  378.1 0.2 copy.34
  378.4 1.3 fusion.12
  379.6 0.2 copy_multiply_fusion
  379.9 2.9 convolution_bitcast_fusion.3
  382.7 1.1 fusion.17
  383.9 1.0 fusion.10
  384.9 1.2 fusion.13
  386.2 0.3 copy.30
  386.5 38.7 %all-gather.11.cloned.1.call-done = bf16[1024,4096]{1,0:T(8,128)(2,1)} async-done(((bf16[1024,512]{1,0:T(8,128)(2,1)}), bf16[1024,4096]{1,0:T(8,128)(2,1)}) %all-gather.11.cloned.1.call-update) | async-done | bytes 8388624 | tf_op jit(solution)/shard_map/all_gather | solution.py:70
  425.3 7.7 %fusion.28 = f32[256,4096]{1,0:T(8,128)} fusion(bf16[1024,4096]{1,0:T(8,128)(2,1)} %all-gather.11.cloned.1.call-done, bf16[32,8,8,128]{3,2,1,0:T(8,128)(2,1)S(1)} %bitcast.140), kind=kOutput, calls=%fused_computation.38 | convolution fusion | flops 2147483648 | bytes 13107200 | tf_op jit(solution)/shard_map/dot_general | solution.py:68
  433.0 1.1 fusion.19
  434.2 1.8 fusion.11
  436.0 48.3 %reduce-scatter.2.cloned.1.call-done = f32[256,1024]{1,0:T(8,128)} async-done(((f32[256,4096]{1,0:T(8,128)}), f32[256,1024]{1,0:T(8,128)}) %reduce-scatter.2.cloned.1.call-update) | async-done | bytes 1048592 | tf_op jit(solution)/shard_map/reduce_scatter | solution.py:73
  484.3 2.2 fusion.27
  (38 shorter events, 0.8 us)
Async XLA Ops:
  7.2 334.9 %all-gather.5.cloned.1.call-start = ((), (), s32[]{:S(2)}) async-start(), calls=%async_computation.2 | async-start | bytes 2621440 | tf_op jit(solution)/shard_map/all_gather | solution.py:33
  7.9 352.4 %all-gather.9.cloned.1.call-start = ((), (), s32[]{:S(2)}) async-start(), calls=%async_computation.4 | async-start | bytes 9437184 | tf_op jit(solution)/shard_map/all_gather | solution.py:55
  8.6 363.5 %all-gather.7.cloned.1.call-start = ((), (), s32[]{:S(2)}) async-start(), calls=%async_computation.3 | async-start | bytes 9437184 | tf_op jit(solution)/shard_map/all_gather | solution.py:43
  14.9 7.1 %copy-start.6 = (s32[1,2,64]{2,1,0:T(2,128)S(1)}, s32[1,2,64]{2,1,0:T(2,128)}, u32[]{:S(2)}) copy-start(s32[1,2,64]{2,1,0:T(2,128)} %param.14) | copy-start | bytes 1540
  14.9 7.4 %copy-start.5 = (bf16[512,8]{0,1:T(8,128)(2,1)S(1)}, bf16[512,8]{0,1:T(8,128)(2,1)}, u32[]{:S(2)}) copy-start(bf16[512,8]{0,1:T(8,128)(2,1)} %param.12) | copy-start | bytes 24580
  14.9 339.5 %all-to-all-start = ((bf16[8,512,1024]{2,1,0:T(8,128)(2,1)}), bf16[8,512,1024]{2,1,0:T(8,128)(2,1)}, u32[]{:S(2)}, u32[]{:S(2)}) async-start(bf16[8,512,1024]{2,1,0:T(8,128)(2,1)} %tile.2), calls=%async_computation | async-start | bytes 16777216 | tf_op jit(solution)/shard_map/all_to_all | solution.py:50
  21.4 403.9 %all-gather.11.cloned.1.call-start = ((), (), s32[]{:S(2)}) async-start(), calls=%async_computation.5 | async-start | bytes 9437184 | tf_op jit(solution)/shard_map/all_gather | solution.py:70
  22.0 462.3 %reduce-scatter.2.cloned.1.call-start = ((), (), s32[]{:S(2)}) async-start(), calls=%async_computation.6 | async-start | bytes 5242880 | tf_op jit(solution)/shard_map/reduce_scatter | solution.py:73
  359.2 0.8 copy-start.2
  372.1 6.2 %copy-start.1 = (f32[1,8,128,128]{3,2,1,0:T(8,128)S(1)}, f32[1,8,128,128]{3,2,1,0:T(8,128)}, u32[]{:S(2)}) copy-start(f32[1,8,128,128]{3,2,1,0:T(8,128)} %param.15) | copy-start | bytes 1572868
  372.1 7.5 %copy-start.3 = (f32[16,8,8,128]{3,2,1,0:T(8,128)S(1)}, f32[16,8,8,128]{3,2,1,0:T(8,128)}, u32[]{:S(2)}) copy-start(f32[16,8,8,128]{3,2,1,0:T(8,128)} %copy-done.2) | copy-start | bytes 1572868
  372.1 7.7 %copy-start = (bf16[1024,4096]{1,0:T(8,128)(2,1)S(1)}, bf16[1024,4096]{1,0:T(8,128)(2,1)}, u32[]{:S(2)}) copy-start(bf16[1024,4096]{1,0:T(8,128)(2,1)} %copy.27) | copy-start | bytes 25165828
  425.3 59.0 %copy-start.4 = (bf16[1,256,1024]{2,1,0:T(8,128)(2,1)S(1)}, bf16[1,256,1024]{2,1,0:T(8,128)(2,1)}, u32[]{:S(2)}) copy-start(bf16[1,256,1024]{2,1,0:T(8,128)(2,1)} %param.8) | copy-start | bytes 1572868
Sparse Core Ops, SparseCore 0:
  9.8 37.8 all-gather.4
  49.4 187.8 all-gather.8
  238.8 103.8 all-gather.6
  344.2 81.0 all-gather.10
  433.2 51.0 reduce-scatter.1
